TPU v7x, 256 devices: a whole 4x4x8 slice. The times are simulated.
256 devices in a mesh: row: 32 (over z, x), col: 4 (over y), rep: 2 (over core).
Axes of the slice: x: 4, y: 4, z: 8, core: 2. Of those that a mesh axis runs over, the one named last changes fastest.
Arguments:
- amplitudes: bfloat16 [32768, 8192], P('row', ('rep', 'col')), may hold values from -6 to 6
- integrals: bfloat16 [8192, 4096], P(('rep', 'row'), 'col'), may hold values from -0.1875 to 0.1875
- tile_mask: int32 [64, 32], replicated, may hold values from 0 to 1
- k_irrep: int32 [64], replicated, may hold values from 0 to 3
- n_irrep: int32 [32], replicated, may hold values from 0 to 3
- stored_tile: int32 [64], replicated, may hold values from 0 to 63, as said below
Outputs:
- ladder: bfloat16 [32768, 4096], P('row', ('col', 'rep'))
Inputs may be any that keep to these rules, and one draw needn't show every extreme that they name: `stored_tile`: for each q, slots q * 32 to (q + 1) * 32 - 1 hold a permutation of the tiles q * 32 to (q + 1) * 32 - 1.
All inputs are finite; a program needn't handle non-finite values.
Results may differ from a plain program's by a relative error of at most 0.001.
Values may be sent and summed in bfloat16 or wider, within the bound.
No kernel may reach another device: no remote copies, remote signals or barrier semaphores. Data moves between devices by JAX's collectives and lax.ppermute only.
A program may use at most 128 MiB of HBM per device.

v0:
```python
import jax
import jax.numpy as jnp
from jax import lax
from jax.sharding import PartitionSpec as P

TS = 128


def on_device(amplitudes, integrals, tile_mask, k_irrep, n_irrep, stored_tile):
    slab = lax.axis_index("rep")
    column = lax.axis_index("col")
    ncol = integrals.shape[1]
    tiles_col = ncol // TS
    n_labels = lax.dynamic_slice_in_dim(n_irrep, column * tiles_col, tiles_col)
    mask_cols = lax.dynamic_slice_in_dim(tile_mask, column * tiles_col, tiles_col, 1)
    stored_rows = integrals.shape[0]
    kq = stored_rows * lax.axis_size("row")
    slab_tiles = kq // TS
    slots = lax.dynamic_slice_in_dim(stored_tile, slab * slab_tiles, slab_tiles)
    gathered = lax.all_gather(integrals, "row", axis=0, tiled=True)
    same = jnp.take(k_irrep, slots)[:, None] == n_labels[None, :]
    occupied = jnp.take(mask_cols, slots, axis=0) == 1
    weights = jnp.logical_and(same, occupied).astype(jnp.bfloat16)
    shaped = gathered.reshape(slab_tiles, TS, tiles_col, TS) * weights[:, None, :, None]
    masked = shaped.reshape(kq, ncol)
    amp_slab = lax.all_gather(amplitudes, "col", axis=1, tiled=True)
    mrow = amp_slab.shape[0]
    local_ids = slots - slab * slab_tiles
    ordered = jnp.take(amp_slab.reshape(mrow, slab_tiles, TS), local_ids, axis=1).reshape(mrow, kq)
    partial_value = jnp.dot(ordered, masked, preferred_element_type=jnp.float32)
    return lax.psum_scatter(partial_value, "rep", scatter_dimension=1, tiled=True).astype(
        jnp.bfloat16
    )


def solution(mesh):
    placed = (P("row", ("rep", "col")), P(("rep", "row"), "col"), P(), P(), P(), P())
    return jax.shard_map(
        on_device, mesh=mesh, in_specs=placed, out_specs=P("row", ("col", "rep")), check_vma=False
    )
```

profile of v0, /device:TPU:1, one launch (start us, length us, event | category | flops | bytes accessed | tf_op | source)
XLA Modules:
  0.0 242.3 jit_solution(16062950526228524270)
XLA Ops:
  6.5 0.0 copy-start
  6.5 0.0 all-gather.3.cloned.1.call-start
  6.5 3.9 %copy.13 = bf16[1024,1024]{0,1:T(8,128)(2,1)} copy(bf16[1024,1024]{1,0:T(8,128)(2,1)} %param.6) | data formatting | bytes 4194304 | tf_op args[0]
  10.5 0.0 all-gather.3.cloned.1.call-update
  10.5 0.0 all-gather.5.cloned.1.call-start
  10.6 0.7 all-gather.5.cloned.1.call-update
  11.3 0.0 reduce-scatter.2.cloned.1.call-start
  11.3 0.7 dynamic_slice.10
  12.0 0.0 copy-done
  12.0 0.1 copy.19
  12.1 0.7 compare_and_fusion
  12.9 1.4 gather_fusion.1
  14.2 0.6 gather_fusion.2
  14.8 0.1 copy.17
  14.9 0.1 fusion.3
  15.0 0.1 copy.18
  15.1 0.1 broadcast_bitcast_fusion
  15.1 84.8 %all-gather.3.cloned.1.call-done = bf16[1024,4096]{0,1:T(8,128)(2,1)} async-done(((bf16[1024,1024]{0,1:T(8,128)(2,1)}), bf16[1024,4096]{0,1:T(8,128)(2,1)}) %all-gather.3.cloned.1.call-update) | async-done | bytes 8388624 | tf_op jit(solution)/shard_map/all_gather | solution.py:26
  99.9 12.0 %copy.14 = bf16[1024,32,128]{2,0,1:T(8,128)(2,1)} copy(bf16[1024,32,128]{0,2,1:T(8,128)(2,1)} %bitcast.14) | data formatting | bytes 16777216 | tf_op jit(solution)/shard_map/reshape | solution.py:29
  111.9 8.4 %gather_fusion = bf16[32,1024,128]{2,1,0:T(8,128)(2,1)} fusion(bf16[1024,32,128]{2,0,1:T(8,128)(2,1)} %copy.14, s32[1024]{0:T(1024)S(1)} %pad_clamp_fusion.1), kind=kCustom, calls=%fused_computation | custom fusion | bytes 16777344 | tf_op jit(solution)/shard_map/jit(_take)/gather | solution.py:29
  120.3 12.0 %copy.15 = bf16[1024,32,128]{0,2,1:T(8,128)(2,1)} copy(bf16[1024,32,128]{2,0,1:T(8,128)(2,1)} %bitcast.12) | data formatting | bytes 16777216 | tf_op jit(solution)/shard_map/jit(_take)/gather | solution.py:29
  132.3 7.3 %bitcast_select_fusion = bf16[1024,4096]{0,1:T(8,128)(2,1)} fusion(bf16[1024,32,128]{0,2,1:T(8,128)(2,1)} %copy.15, pred[4096]{0:T(1024)(128)(4,1)S(1)} %broadcast_bitcast_fusion), kind=kLoop, calls=%fused_computation.6 | loop fusion | flops 4194304 | bytes 16781312 | tf_op jit(solution)/shard_map/jit(_take)/select_n | solution.py:29
  139.6 61.2 %all-gather.5.cloned.1.call-done = bf16[4096,1024]{1,0:T(8,128)(2,1)} async-done(((bf16[128,1024]{1,0:T(8,128)(2,1)}), bf16[4096,1024]{1,0:T(8,128)(2,1)}) %all-gather.5.cloned.1.call-update) | async-done | bytes 8388624 | tf_op jit(solution)/shard_map/all_gather | solution.py:20
  200.8 0.0 copy-start.2
  200.8 1.1 mul.21
  201.9 2.2 copy-done.2
  204.2 0.0 copy-start.1
  204.2 13.0 %fusion = f32[1024,1024]{1,0:T(8,128)} fusion(bf16[1024,4096]{0,1:T(8,128)(2,1)S(1)} %copy-done.2, bf16[4096,1024]{1,0:T(8,128)(2,1)} %all-gather.5.cloned.1.call-done, bf16[512,8,8,128]{3,2,1,0:T(8,128)(2,1)S(1)} %bitcast.13), kind=kOutput, calls=%fused_computation.4 | convolution fusion | flops 8594128896 | bytes 29360128 | tf_op jit(solution)/shard_map/dot_general | solution.py:30
  217.1 0.0 reduce-scatter.2.cloned.1.call-update
  217.1 16.0 %reduce-scatter.2.cloned.1.call-done = f32[1024,512]{1,0:T(8,128)} async-done(((f32[1024,1024]{1,0:T(8,128)}), f32[1024,512]{1,0:T(8,128)}) %reduce-scatter.2.cloned.1.call-update) | async-done | bytes 2097168 | tf_op jit(solution)/shard_map/reduce_scatter | solution.py:31
  233.1 2.7 %convert_element_type.11 = bf16[1024,512]{1,0:T(8,128)(2,1)} convert(f32[1024,512]{1,0:T(8,128)} %reduce-scatter.2.cloned.1.call-done) | non-fusion elementwise | flops 524288 | bytes 3145728 | tf_op jit(solution)/shard_map/convert_element_type | solution.py:31
  235.8 0.0 copy-done.1
  (4 shorter events, 0.0 us)
Async XLA Ops:
  6.5 5.5 %copy-start = (s32[64,32]{0,1:T(8,128)S(1)}, s32[64,32]{0,1:T(8,128)}, u32[]{:S(2)}) copy-start(s32[64,32]{0,1:T(8,128)} %param.8) | copy-start | bytes 24580
  6.5 93.4 %all-gather.3.cloned.1.call-start = ((), (), s32[]{:S(2)}) async-start(), calls=%async_computation.1 | async-start | bytes 10485760 | tf_op jit(solution)/shard_map/all_gather | solution.py:26
  10.5 190.3 %all-gather.5.cloned.1.call-start = ((), (), s32[]{:S(2)}) async-start(), calls=%async_computation.2 | async-start | bytes 8650752 | tf_op jit(solution)/shard_map/all_gather | solution.py:20
  11.3 221.9 %reduce-scatter.2.cloned.1.call-start = ((), (), s32[]{:S(2)}) async-start(), calls=%async_computation.3 | async-start | bytes 6291456 | tf_op jit(solution)/shard_map/reduce_scatter | solution.py:31
  200.8 3.4 %copy-start.2 = (bf16[1024,4096]{0,1:T(8,128)(2,1)S(1)}, bf16[1024,4096]{0,1:T(8,128)(2,1)}, u32[]{:S(2)}) copy-start(bf16[1024,4096]{0,1:T(8,128)(2,1)} %bitcast_select_fusion) | copy-start | bytes 25165828
  204.2 31.7 %copy-start.1 = (s32[64,32]{0,1:T(8,128)S(1)}, s32[64,32]{0,1:T(8,128)}, u32[]{:S(2)}) copy-start(s32[64,32]{0,1:T(8,128)} %param.8) | copy-start | bytes 24580
Sparse Core Ops, SparseCore 0:
  10.6 89.2 all-gather.2
  102.5 98.2 all-gather.4
  217.3 15.8 reduce-scatter.1
where the time goes:
time: 243 us; the launch traced here: 242 us
  waiting for transfers between devices  163 us (67%)
  local copies, waits for them, and re-layouts  42.7 us (18%)
  between operations  13.1 us (5%)
  matrix products  13 us (5%)
  other arithmetic  10.8 us (4%)
    all_gather x1, waiting for transfers between devices, on_device(): amp_slab = lax.all_gather(amplitudes, 'col', axis=1, tiled=True)  84.8 us
    all_gather x1, waiting for transfers between devices, on_device(): gathered = lax.all_gather(integrals, 'row', axis=0, tiled=True)  61.2 us
    gather x2, local copies, waits for them, and re-layouts, on_device(): jnp.take(amp_slab.reshape(mrow, slab_tiles, TS), local_ids, axis=1)  20.4 us
    reduce_scatter x1, waiting for transfers between devices, on_device(): lax.psum_scatter(partial_value, 'rep', scatter_dimension=1, tiled=True)  16 us
    dot_general x1, matrix products, on_device(): partial_value = jnp.dot(ordered, masked, preferred_element_type=jnp.float32)  13 us
    reshape x1, local copies, waits for them, and re-layouts, on_device(): amp_slab.reshape(mrow, slab_tiles, TS)  12 us
    select_n x1, other arithmetic, on_device(): jnp.take(amp_slab.reshape(mrow, slab_tiles, TS), local_ids, axis=1)  7.27 us
    unnamed x8, local copies, waits for them, and re-layouts  6.26 us
  transfers between devices with their start and end apart: 3, of which 3 were waited for; matrix products, arithmetic and copies ran while one was open for 18% of the time, Pallas kernels for 0%

commit v1 on v0

--- a/solution.py
+++ b/solution.py
@@ -23,7 +23,9 @@
     weights = jnp.logical_and(same, occupied).astype(jnp.bfloat16)
     shaped = gathered.reshape(slab_tiles, TS, tiles_col, TS) * weights[:, None, :, None]
     masked = shaped.reshape(kq, ncol)
-    amp_slab = lax.all_gather(amplitudes, "col", axis=1, tiled=True)
+    amp_slab = jnp.concatenate(
+        lax.all_to_all(jnp.stack([amplitudes] * lax.axis_size("col")), "col", 0, 0), axis=1
+    )
     mrow = amp_slab.shape[0]
     local_ids = slots - slab * slab_tiles
     ordered = jnp.take(amp_slab.reshape(mrow, slab_tiles, TS), local_ids, axis=1).reshape(mrow, kq)

time: 243 us -> 201 us (0.83)
  waiting for transfers between devices: 163 us -> 113 us
  starting transfers between devices: 0.08 us -> 5.84 us
    all_to_all x0 -> x1, waiting for transfers between devices: none -> 90.2 us  [on_device(): lax.all_to_all(jnp.stack([amplitudes] * lax.axis_size('col')), 'col', 0, 0)]
    all_gather x1 -> x0, waiting for transfers between devices: 84.8 us -> none  [on_device(): amp_slab = lax.all_gather(amplitudes, 'col', axis=1, tiled=True)]
    all_gather x1, waiting for transfers between devices: 61.2 us -> 0.01 us  [on_device(): gathered = lax.all_gather(integrals, 'row', axis=0, tiled=True)]
    another operation x0 -> x2, local copies, waits for them, and re-layouts: none -> 16.3 us  [the longest x1 12 us: on_device(): amp_slab.reshape(mrow, slab_tiles, TS)]
    reshape x1 -> x0, local copies, waits for them, and re-layouts: 12 us -> none  [on_device(): amp_slab.reshape(mrow, slab_tiles, TS)]
    reduce_scatter x1, waiting for transfers between devices: 16 us -> 21.9 us  [on_device(): lax.psum_scatter(partial_value, 'rep', scatter_dimension=1, tiled=True)]
    all_to_all x0 -> x1, starting transfers between devices: none -> 5.8 us  [on_device(): lax.all_to_all(jnp.stack([amplitudes] * lax.axis_size('col')), 'col', 0, 0)]
    unnamed x8 -> x14, local copies, waits for them, and re-layouts: 6.26 us -> 5.2 us
  transfers between devices with their start and end apart: 3 -> 3, of which waited for: 3 -> 2; matrix products, arithmetic and copies ran while one was open for 18% -> 24% of each run, Pallas kernels for 0% -> 0%
where the time goes in v1:
time: 201 us; the launch traced here: 200 us
  waiting for transfers between devices  113 us (56%)
  local copies, waits for them, and re-layouts  44.6 us (22%)
  between operations  13.5 us (7%)
  matrix products  12.9 us (6%)
  other arithmetic  10.1 us (5%)
  starting transfers between devices  5.84 us (3%)
    all_to_all x1, waiting for transfers between devices, on_device(): lax.all_to_all(jnp.stack([amplitudes] * lax.axis_size('col')), 'col', 0, 0)  90.2 us
    reduce_scatter x1, waiting for transfers between devices, on_device(): lax.psum_scatter(partial_value, 'rep', scatter_dimension=1, tiled=True)  21.9 us
    gather x2, local copies, waits for them, and re-layouts, on_device(): jnp.take(amp_slab.reshape(mrow, slab_tiles, TS), local_ids, axis=1)  20.4 us
    dot_general x1, matrix products, on_device(): partial_value = jnp.dot(ordered, masked, preferred_element_type=jnp.float32)  12.9 us
    another operation x1, local copies, waits for them, and re-layouts, on_device(): amp_slab.reshape(mrow, slab_tiles, TS)  12 us
    select_n x1, other arithmetic, on_device(): jnp.take(amp_slab.reshape(mrow, slab_tiles, TS), local_ids, axis=1)  7.25 us
    all_to_all x1, starting transfers between devices, on_device(): lax.all_to_all(jnp.stack([amplitudes] * lax.axis_size('col')), 'col', 0, 0)  5.8 us
    unnamed x14, local copies, waits for them, and re-layouts  5.2 us
  transfers between devices with their start and end apart: 3, of which 2 were waited for; matrix products, arithmetic and copies ran while one was open for 24% of the time, Pallas kernels for 0%

profile of v1, /device:TPU:1, one launch (start us, length us, event | category | flops | bytes accessed | tf_op | source)
XLA Modules:
  0.0 199.8 jit_solution(5010650711979478620)
XLA Ops:
  6.5 0.0 copy-start
  6.5 0.0 all-gather.2.cloned.1.call-start
  6.5 0.7 all-gather.2.cloned.1.call-update
  7.3 2.9 %copy.15 = bf16[1024,1024]{0,1:T(8,128)(2,1)S(1)} copy(bf16[1024,1024]{1,0:T(8,128)(2,1)} %param.6) | data formatting | bytes 4194304 | tf_op args[0]
  10.1 4.3 %stack.2 = bf16[4,1024,1024]{1,2,0:T(8,128)(2,1)} broadcast(bf16[1024,1024]{0,1:T(8,128)(2,1)S(1)} %copy.15), dimensions={1,2} | broadcast | bytes 10485760 | tf_op jit(solution)/shard_map/stack | solution.py:27
  14.4 0.0 copy-start.5
  14.4 0.0 copy-start.4
  14.5 0.0 copy-start.2
  14.5 5.8 %all-to-all-start = ((bf16[4,1024,1024]{1,2,0:T(8,128)(2,1)}), bf16[4,1024,1024]{1,2,0:T(8,128)(2,1)}, u32[]{:S(2)}, u32[]{:S(2)}) async-start(bf16[4,1024,1024]{1,2,0:T(8,128)(2,1)} %stack.2), calls=%async_computation | async-start | bytes 16777216 | tf_op jit(solution)/shard_map/all_to_all | solution.py:27
  20.3 0.0 reduce-scatter.2.cloned.1.call-start
  20.3 0.0 copy-done.5
  20.3 0.1 dynamic_slice.10
  20.4 0.0 copy-done
  20.4 0.1 copy.21
  20.5 0.0 copy-done.4
  20.5 0.1 compare_and_fusion
  20.6 0.0 copy-done.2
  20.6 0.7 gather_fusion.1
  21.3 0.6 gather_fusion.2
  21.9 0.1 copy.19
  22.0 0.1 fusion.3
  22.0 0.1 copy.20
  22.1 0.1 broadcast_bitcast_fusion
  22.2 90.2 %all-to-all-done = bf16[4,1024,1024]{1,2,0:T(8,128)(2,1)} async-done(((bf16[4,1024,1024]{1,2,0:T(8,128)(2,1)}), bf16[4,1024,1024]{1,2,0:T(8,128)(2,1)}, u32[]{:S(2)}, u32[]{:S(2)}) %all-to-all-start) | async-done | bytes 8388640 | tf_op jit(solution)/shard_map/all_to_all | solution.py:27
  112.4 12.0 %copy.16 = bf16[1024,32,128]{2,0,1:T(8,128)(2,1)} copy(bf16[1024,32,128]{0,2,1:T(8,128)(2,1)} %bitcast.2) | data formatting | bytes 16777216 | tf_op jit(solution)/shard_map/reshape;reshape | solution.py:31
  124.4 8.4 %gather_fusion = bf16[32,1024,128]{2,1,0:T(8,128)(2,1)} fusion(bf16[1024,32,128]{2,0,1:T(8,128)(2,1)} %copy.16, s32[1024]{0:T(1024)S(1)} %pad_clamp_fusion.1), kind=kCustom, calls=%fused_computation | custom fusion | bytes 16777344 | tf_op jit(solution)/shard_map/jit(_take)/gather | solution.py:31
  132.8 12.0 %copy.17 = bf16[1024,32,128]{0,2,1:T(8,128)(2,1)} copy(bf16[1024,32,128]{2,0,1:T(8,128)(2,1)} %bitcast.14) | data formatting | bytes 16777216 | tf_op jit(solution)/shard_map/jit(_take)/gather | solution.py:31
  144.8 7.2 %bitcast_select_fusion = bf16[1024,4096]{0,1:T(8,128)(2,1)} fusion(bf16[1024,32,128]{0,2,1:T(8,128)(2,1)} %copy.17, pred[4096]{0:T(1024)(128)(4,1)S(1)} %broadcast_bitcast_fusion), kind=kLoop, calls=%fused_computation.6 | loop fusion | flops 4194304 | bytes 16781312 | tf_op jit(solution)/shard_map/jit(_take)/select_n | solution.py:31
  152.0 0.0 all-gather.2.cloned.1.call-done
  152.0 0.0 copy-start.3
  152.0 1.1 mul.21
  153.2 2.2 %copy-done.3 = bf16[1024,4096]{0,1:T(8,128)(2,1)S(1)} copy-done((bf16[1024,4096]{0,1:T(8,128)(2,1)S(1)}, bf16[1024,4096]{0,1:T(8,128)(2,1)}, u32[]{:S(2)}) %copy-start.3) | copy-done | bytes 8388632
  155.4 0.0 copy-start.1
  155.4 12.9 %fusion = f32[1024,1024]{1,0:T(8,128)} fusion(bf16[1024,4096]{0,1:T(8,128)(2,1)S(1)} %copy-done.3, bf16[4096,1024]{1,0:T(8,128)(2,1)} %all-gather.2.cloned.1.call-done, bf16[512,8,8,128]{3,2,1,0:T(8,128)(2,1)S(1)} %bitcast.15), kind=kOutput, calls=%fused_computation.4 | convolution fusion | flops 8594128896 | bytes 29360128 | tf_op jit(solution)/shard_map/dot_general | solution.py:32
  168.3 0.0 reduce-scatter.2.cloned.1.call-update
  168.4 21.9 %reduce-scatter.2.cloned.1.call-done = f32[1024,512]{1,0:T(8,128)} async-done(((f32[1024,1024]{1,0:T(8,128)}), f32[1024,512]{1,0:T(8,128)}) %reduce-scatter.2.cloned.1.call-update) | async-done | bytes 2097168 | tf_op jit(solution)/shard_map/reduce_scatter | solution.py:33
  190.2 2.7 %convert_element_type.11 = bf16[1024,512]{1,0:T(8,128)(2,1)} convert(f32[1024,512]{1,0:T(8,128)} %reduce-scatter.2.cloned.1.call-done) | non-fusion elementwise | flops 524288 | bytes 3145728 | tf_op jit(solution)/shard_map/convert_element_type | solution.py:33
  192.9 0.0 copy-done.1
  (4 shorter events, 0.0 us)
Async XLA Ops:
  6.5 13.9 %copy-start = (s32[64,32]{0,1:T(8,128)S(1)}, s32[64,32]{0,1:T(8,128)}, u32[]{:S(2)}) copy-start(s32[64,32]{0,1:T(8,128)} %param.8) | copy-start | bytes 24580
  6.5 145.5 %all-gather.2.cloned.1.call-start = ((), (), s32[]{:S(2)}) async-start(), calls=%async_computation.2 | async-start | bytes 8650752 | tf_op jit(solution)/shard_map/all_gather | solution.py:20
  14.4 5.9 %copy-start.5 = (s32[32]{0:T(128)S(1)}, s32[32]{0:T(128)}, u32[]{:S(2)}) copy-start(s32[32]{0:T(128)} %param.10) | copy-start | bytes 388
  14.4 6.0 %copy-start.4 = (s32[64]{0:T(128)S(1)}, s32[64]{0:T(128)}, u32[]{:S(2)}) copy-start(s32[64]{0:T(128)} %param.11) | copy-start | bytes 772
  14.5 6.1 %copy-start.2 = (s32[64]{0:T(128)S(1)}, s32[64]{0:T(128)}, u32[]{:S(2)}) copy-start(s32[64]{0:T(128)} %param.9) | copy-start | bytes 772
  14.5 97.9 %all-to-all-start = ((bf16[4,1024,1024]{1,2,0:T(8,128)(2,1)}), bf16[4,1024,1024]{1,2,0:T(8,128)(2,1)}, u32[]{:S(2)}, u32[]{:S(2)}) async-start(bf16[4,1024,1024]{1,2,0:T(8,128)(2,1)} %stack.2), calls=%async_computation | async-start | bytes 16777216 | tf_op jit(solution)/shard_map/all_to_all | solution.py:27
  20.3 170.0 %reduce-scatter.2.cloned.1.call-start = ((), (), s32[]{:S(2)}) async-start(), calls=%async_computation.3 | async-start | bytes 6291456 | tf_op jit(solution)/shard_map/reduce_scatter | solution.py:33
  152.0 3.4 %copy-start.3 = (bf16[1024,4096]{0,1:T(8,128)(2,1)S(1)}, bf16[1024,4096]{0,1:T(8,128)(2,1)}, u32[]{:S(2)}) copy-start(bf16[1024,4096]{0,1:T(8,128)(2,1)} %bitcast_select_fusion) | copy-start | bytes 25165828
  155.4 37.5 %copy-start.1 = (s32[64,32]{0,1:T(8,128)S(1)}, s32[64,32]{0,1:T(8,128)}, u32[]{:S(2)}) copy-start(s32[64,32]{0,1:T(8,128)} %param.8) | copy-start | bytes 24580
Sparse Core Ops, SparseCore 0:
  9.9 100.8 all-gather.1
  168.5 21.6 reduce-scatter.1
